TPU v7x, 256 devices: a whole 4x4x8 slice. The times are simulated.
256 devices in a mesh: wide: 32 (over z_hi, y, x), narrow: 8 (over z_lo, core).
Axes of the slice: x: 4, y: 4, z: 8 (z_hi: 2, z_lo: 4; z = z_hi * 4 + z_lo), core: 2. Of those that a mesh axis runs over, the one named last changes fastest.
Arguments:
- tile_pool: bfloat16 [32, 1024, 768], P('wide', 'narrow'), may hold values from -96 to 96
- batch_index: int32 [32, 2048], P('wide', 'narrow'), may hold values from 0 to 127
- pair_label: int32 [32, 2048], P('wide', 'narrow'), may hold values from 0 to 255, as said below
- w_first: bfloat16 [768, 2048], P('narrow'), may hold values from -0.375 to 0.375
- w_second: bfloat16 [2048, 2048], P('narrow'), may hold values from -0.375 to 0.375
- m_first: bfloat16 [32, 768, 2048], P('wide', 'narrow'), may hold values from -0.01275776 to 0.01275776
- m_second: bfloat16 [32, 2048, 2048], P('wide', 'narrow'), may hold values from -0.0078125 to 0.0078125
- v_first: bfloat16 [32, 768, 2048], P('wide', 'narrow'), may hold values from 0.0005086263 to 0.025431315
- v_second: bfloat16 [32, 2048, 2048], P('wide', 'narrow'), may hold values from 0.00019073486 to 0.009536743
- mom_first: bfloat16 [768, 2048], P('narrow'), may hold values from -0.1796875 to 0.1796875
- mom_second: bfloat16 [2048, 2048], P('narrow'), may hold values from -0.1796875 to 0.1796875
Outputs:
- new_first: bfloat16 [768, 2048], P('narrow')
- new_second: bfloat16 [2048, 2048], P('narrow')
- mom_out_first: bfloat16 [768, 2048], P('narrow')
- mom_out_second: bfloat16 [2048, 2048], P('narrow')
Inputs may be any that keep to these rules, and one draw needn't show every extreme that they name: `batch_index`: indices count within the pool of the same site and shard. `pair_label`: each row's partner is another row of the same site and shard, counted within that shard's 256 rows, and names the row back.
All inputs are finite; a program needn't handle non-finite values.
Results may differ from a plain program's by a relative error of at most 0.0075.
Values may be sent and summed in bfloat16 or wider, within the bound.
A program may use at most 128 MiB of HBM per device.

v0:
```python
import math
import jax
import jax.numpy as jnp
import numpy as np
from jax import lax
from jax.sharding import Mesh
from jax.sharding import PartitionSpec as P

PIX = 768
MID = 2048
OUT = 2048
logit_scale = 1.0 / 0.07
rate_inner = 0.2
weight_decay = 0.1
beta_first = 0.9
beta_second = 0.95
adam_eps = 1e-08
rate_outer = 0.7
momentum_coef = 0.9
WIDE = ("zh", "y", "x")
NARROW = ("zl", "c")


def adam_delta(grads, first_moment, second_moment, weights):
    moment_one = beta_first * first_moment.astype(jnp.float32) + (1.0 - beta_first) * grads
    moment_two = (
        beta_second * second_moment.astype(jnp.float32) + (1.0 - beta_second) * grads * grads
    )
    return rate_inner * (
        moment_one / (jnp.sqrt(moment_two) + adam_eps) + weight_decay * weights.astype(jnp.float32)
    )


def outer_update(delta, momentum, weights):
    velocity = momentum_coef * momentum.astype(jnp.float32) + delta
    updated = weights.astype(jnp.float32) - rate_outer * (delta + momentum_coef * velocity)
    return (updated.astype(jnp.bfloat16), velocity.astype(jnp.bfloat16))


def embed_gradient(embedded, partner):
    inverse = lax.rsqrt(jnp.sum(embedded * embedded, axis=1, keepdims=True) + OUT * 1e-06)
    unit_rows = embedded * inverse
    unit_half = unit_rows.astype(jnp.bfloat16)
    scores = logit_scale * jnp.dot(unit_half, unit_half.T, preferred_element_type=jnp.float32)
    positions = jnp.arange(embedded.shape[0], dtype=jnp.int32)
    diagonal = positions[:, None] == positions[None, :]
    scores = jnp.where(diagonal, -1e30, scores)
    highest = jnp.max(scores, axis=1, keepdims=True)
    powers = jnp.exp(scores - highest)
    softmax_rows = powers / jnp.sum(powers, axis=1, keepdims=True)
    target = (partner[:, None] == positions[None, :]).astype(jnp.float32)
    score_grad = softmax_rows - target
    paired = (score_grad + score_grad.T).astype(jnp.bfloat16)
    unit_grad = logit_scale * jnp.dot(paired, unit_half, preferred_element_type=jnp.float32)
    embed_grad = inverse * (
        unit_grad - unit_rows * jnp.sum(unit_rows * unit_grad, axis=1, keepdims=True)
    )
    return embed_grad.astype(jnp.bfloat16)


def plane_sum(delta):
    plane = ("y", "x")
    n_plane = lax.axis_size(plane)
    rows, cols = delta.shape
    got = lax.all_to_all(delta, plane, 1, 0, tiled=True)
    return jnp.sum(got.reshape(n_plane, rows, cols // n_plane), axis=0)


def wide_mean_update(delta, momentum, weights, part=None):
    plane = ("y", "x")
    n_plane = lax.axis_size(plane)
    n_half = lax.axis_size("zh")
    sites = n_plane * n_half
    rows, cols = momentum.shape
    p1 = cols // n_plane
    p2 = p1 // n_half
    part = plane_sum(delta) if part is None else part
    got = lax.all_to_all(part, "zh", 1, 0, tiled=True)
    mean = jnp.sum(got.reshape(n_half, rows, p2), axis=0) / sites
    start = lax.axis_index(plane) * p1 + lax.axis_index("zh") * p2
    mom_piece = lax.dynamic_slice_in_dim(momentum, start, p2, axis=1)
    w_piece = lax.dynamic_slice_in_dim(weights, start, p2, axis=1)
    new_piece, vel_piece = outer_update(mean, mom_piece, w_piece)
    both = jnp.stack([new_piece, vel_piece], axis=0)
    back = lax.all_to_all(
        jnp.broadcast_to(both[None], (n_half,) + both.shape), "zh", 0, 0, tiled=True
    )
    back = back.transpose(1, 2, 0, 3).reshape(2, rows, p1)
    back = lax.all_to_all(
        jnp.broadcast_to(back[None], (n_plane,) + back.shape), plane, 0, 0, tiled=True
    )
    back = back.transpose(1, 2, 0, 3).reshape(2, rows, cols)
    return (back[0], back[1])


def gather_weights(w_first, w_second):
    halves = lax.axis_size("zh")
    h = lax.axis_index("zh")
    shards_n = lax.axis_size(NARROW)
    r1 = w_first.shape[0] // halves
    r2 = w_second.shape[0] // halves
    mine = jnp.concatenate(
        [
            lax.dynamic_slice_in_dim(w_first, h * r1, r1, axis=0),
            lax.dynamic_slice_in_dim(w_second, h * r2, r2, axis=0),
        ],
        axis=0,
    )
    got = lax.all_gather(mine, ("zh",) + NARROW, axis=0, tiled=False)
    got = got.reshape(halves, shards_n, r1 + r2, got.shape[-1])
    return (got[:, :, :r1], got[:, :, r1:])


def split_rows(x, like):
    halves, shards_n, r = like.shape[:3]
    return x.reshape(x.shape[0], shards_n, halves, r)


def shards(
    tile_pool,
    batch_index,
    pair_label,
    w_first,
    w_second,
    m_first,
    m_second,
    v_first,
    v_second,
    mom_first,
    mom_second,
):
    inputs = jnp.take(tile_pool[0], batch_index[0], axis=0)
    partner = pair_label[0]
    scale_one = 1.0 / math.sqrt(PIX)
    scale_two = 1.0 / math.sqrt(MID)
    first_whole, second_whole = gather_weights(w_first, w_second)
    hidden = (
        jnp.einsum(
            "bnhr,hnrc->bc",
            split_rows(inputs, first_whole),
            first_whole,
            preferred_element_type=jnp.float32,
        )
        * scale_one
    )
    active_full, gelu_back = jax.vjp(jax.nn.gelu, hidden)
    active = active_full.astype(jnp.bfloat16)
    embedded = (
        jnp.einsum(
            "bnhr,hnrc->bc",
            split_rows(active, second_whole),
            second_whole,
            preferred_element_type=jnp.float32,
        )
        * scale_two
    )
    embed_half = embed_gradient(embedded, partner)
    grad_second = lax.psum_scatter(
        (scale_two * jnp.dot(active.T, embed_half, preferred_element_type=jnp.float32)).astype(
            jnp.bfloat16
        ),
        NARROW,
        scatter_dimension=0,
        tiled=True,
    ).astype(jnp.float32)
    active_grad = scale_two * jnp.einsum(
        "bc,hnrc->bnhr", embed_half, second_whole, preferred_element_type=jnp.float32
    ).reshape(active.shape)
    hidden_half = gelu_back(active_grad)[0].astype(jnp.bfloat16)
    term_first = (
        scale_one * jnp.dot(inputs.T, hidden_half, preferred_element_type=jnp.float32)
    ).astype(jnp.bfloat16)
    term_first, grad_second = lax.optimization_barrier((term_first, grad_second))
    delta_second = adam_delta(grad_second, m_second[0], v_second[0], w_second)
    part_second = plane_sum(delta_second)
    grad_first = lax.psum_scatter(term_first, NARROW, scatter_dimension=0, tiled=True).astype(
        jnp.float32
    )
    delta_first = adam_delta(grad_first, m_first[0], v_first[0], w_first)
    part_first = plane_sum(delta_first)
    rows_first = w_first.shape[0]
    new_w, vel = wide_mean_update(
        None,
        jnp.concatenate([mom_first, mom_second], axis=0),
        jnp.concatenate([w_first, w_second], axis=0),
        jnp.concatenate([part_first, part_second], axis=0),
    )
    return (new_w[:rows_first], new_w[rows_first:], vel[:rows_first], vel[rows_first:])


def solution(mesh):
    zh, y, x = (2, 4, 4)
    devices = np.asarray(mesh.devices)
    wide, narrow = devices.shape
    sub = Mesh(devices.reshape(zh, y, x, narrow // 2, 2), WIDE + NARROW)
    site = P(WIDE, NARROW, None)
    rows = P(NARROW, None)
    return jax.shard_map(
        shards,
        mesh=sub,
        in_specs=(
            site,
            P(WIDE, NARROW),
            P(WIDE, NARROW),
            rows,
            rows,
            site,
            site,
            site,
            site,
            rows,
            rows,
        ),
        out_specs=(rows, rows, rows, rows),
        check_vma=False,
    )
```

profile of v0, /device:TPU:96, one launch (start us, length us, event | category | flops | bytes accessed | tf_op | source)
XLA Modules:
  0.0 355.6 jit_solution(15545826880929783917)
XLA Ops:
  7.2 0.0 copy-start
  7.2 0.0 all-gather.3.cloned.1.call-start
  7.2 1.1 constant_dynamic-slice_fusion
  8.3 0.9 constant_dynamic-slice_fusion.1
  9.3 0.9 pad_maximum_fusion
  10.2 0.0 all-gather.3.cloned.1.call-update
  10.2 0.0 reduce-scatter.3.cloned.1.call-start
  10.3 1.2 gather_fusion
  11.5 0.2 copy.44
  11.7 70.6 %all-gather.3.cloned.1.call-done = bf16[2816,2048]{1,0:T(8,128)(2,1)} async-done(((bf16[176,2048]{1,0:T(8,128)(2,1)}), bf16[2816,2048]{1,0:T(8,128)(2,1)}) %all-gather.3.cloned.1.call-update) | async-done | bytes 11534352 | tf_op jit(solution)/shard_map/all_gather | solution.py:109
  82.3 4.8 %multiply_convert_fusion.3 = (bf16[256,2048]{1,0:T(8,128)(2,1)S(1)}, f32[256,2048]{1,0:T(8,128)}) fusion(bf16[2,8,176,2048]{3,2,1,0:T(8,128)(2,1)} %bitcast.96, bf16[256,8,2,48]{0,3,2,1:T(8,128)(2,1)S(1)} %bitcast.93, pred[256]{0:T(512)(128)(4,1)S(1)} %compare_and_fusion), kind=kOutput, calls=%fused_computation.35 | convolution fusion | flops 810745856 | bytes 6684928 | tf_op jit(solution)/shard_map/bnhr,hnrc->bc/dot_general | solution.py:138
  87.2 1.0 copy-done.6
  88.1 1.5 reshape.106
  89.7 5.2 %multiply_reduce_fusion.1 = (f32[256]{0:T(256)S(1)}, f32[256,2048]{1,0:T(8,128)S(1)}) fusion(bf16[2,8,176,2048]{3,2,1,0:T(8,128)(2,1)} %bitcast.97, bf16[256,8,2,128]{3,2,1,0:T(2,128)(2,1)} %reshape.106), kind=kOutput, calls=%fused_computation.34 | convolution fusion | flops 2149056256 | bytes 11535360 | tf_op jit(solution)/shard_map/bnhr,hnrc->bc/dot_general | solution.py:149
  94.9 0.0 copy-start.11
  94.9 0.6 convolution_multiply_fusion.1
  95.5 0.1 copy.47
  95.6 0.1 fusion.52
  95.7 0.2 fusion.53
  96.0 0.8 multiply_reduce_fusion
  96.7 0.5 multiply_convert_fusion.2
  97.3 0.0 copy-start.8
  97.3 1.0 copy-done.8
  98.2 5.7 %multiply_convert_fusion = bf16[2048,2048]{1,0:T(8,128)(2,1)} fusion(bf16[256,2048]{1,0:T(8,128)(2,1)S(1)} %copy-done.7, bf16[256,2048]{1,0:T(8,128)(2,1)S(1)} %multiply_convert_fusion.2), kind=kOutput, calls=%fused_computation.1 | convolution fusion | flops 2155872256 | bytes 10485760 | tf_op jit(solution)/shard_map/dot_general | solution.py:159
  103.9 0.0 reduce-scatter.3.cloned.1.call-update
  103.9 0.2 reduce-scatter.5.cloned.1.call-start
  104.2 1.0 copy-done.9
  105.1 7.1 %multiply_bitcast_fusion = f32[256,8,2,128]{0,3,1,2:T(8,128)} fusion(bf16[2,8,176,2048]{3,2,1,0:T(8,128)(2,1)} %bitcast.98, bf16[256,2048]{1,0:T(8,128)(2,1)S(1)} %copy-done.9), kind=kOutput, calls=%fused_computation.31 | convolution fusion | flops 2148007936 | bytes 11534336 | tf_op jit(solution)/shard_map/bc,hnrc->bnhr/dot_general | solution.py:166
  112.3 3.4 copy.48
  115.7 2.7 mul.261
  118.3 6.1 %multiply_convert_fusion.1 = bf16[768,2048]{1,0:T(8,128)(2,1)} fusion(f32[256,2048]{1,0:T(8,128)} %get-tuple-element.21, f32[256,2048]{1,0:T(8,128)} %mul.261, bf16[256,768]{1,0:T(8,128)(2,1)S(1)} %gather_fusion, pred[256]{0:T(512)(128)(4,1)S(1)} %compare_and_fusion), kind=kOutput, calls=%fused_computation.6 | convolution fusion | flops 819134464 | bytes 7733504 | tf_op jit(solution)/shard_map/dot_general | solution.py:171
  124.5 70.9 %reduce-scatter.3.cloned.1.call-done = bf16[256,2048]{1,0:T(8,128)(2,1)} async-done(((bf16[2048,2048]{1,0:T(8,128)(2,1)}), bf16[256,2048]{1,0:T(8,128)(2,1)}) %reduce-scatter.3.cloned.1.call-update) | async-done | bytes 1048592 | tf_op jit(solution)/shard_map/reduce_scatter | solution.py:158
  195.4 1.5 convert_element_type.78
  196.8 0.0 copy-start.2
  196.8 0.0 reduce-scatter.5.cloned.1.call-update
  196.9 1.2 copy-done.2
  198.1 4.5 %copy_bitcast_fusion = f32[256,16,128]{2,0,1:T(8,128)} fusion(bf16[256,2048]{1,0:T(8,128)(2,1)S(1)} %copy-done.2, f32[256,2048]{1,0:T(8,128)S(1)} %convert_element_type.78, bf16[1,256,2048]{2,1,0:T(8,128)(2,1)} %param.19, bf16[1,256,2048]{2,1,0:T(8,128)(2,1)} %param.17), kind=kLoop, calls=%fused_computation.29 | loop fusion | flops 7864320 | bytes 7340032 | tf_op jit(solution)/shard_map/all_to_all | solution.py:65
  202.5 6.8 %all-to-all-start.1 = ((f32[256,16,128]{2,0,1:T(8,128)}), f32[256,16,128]{2,0,1:T(8,128)S(1)}, u32[]{:S(2)}, u32[]{:S(2)}) async-start(f32[256,16,128]{2,0,1:T(8,128)} %copy_bitcast_fusion), calls=%async_computation.3 | async-start | bytes 4194304 | tf_op jit(solution)/shard_map/all_to_all | solution.py:65
  209.3 31.8 %reduce-scatter.5.cloned.1.call-done = bf16[96,2048]{1,0:T(8,128)(2,1)} async-done(((bf16[768,2048]{1,0:T(8,128)(2,1)}), bf16[96,2048]{1,0:T(8,128)(2,1)}) %reduce-scatter.5.cloned.1.call-update) | async-done | bytes 393232 | tf_op jit(solution)/shard_map/reduce_scatter | solution.py:176
  241.1 2.8 copy_bitcast_fusion.1
  244.0 6.9 %all-to-all-start = ((f32[96,16,128]{2,0,1:T(8,128)}), f32[96,16,128]{2,0,1:T(8,128)}, u32[]{:S(2)}, u32[]{:S(2)}) async-start(f32[96,16,128]{2,0,1:T(8,128)} %copy_bitcast_fusion.1), calls=%async_computation.2 | async-start | bytes 1572864 | tf_op jit(solution)/shard_map/all_to_all | solution.py:65
  250.9 0.1 reduce_sum.58
  251.0 0.0 copy-start.4
  251.0 14.4 %all-to-all-done = f32[96,16,128]{2,0,1:T(8,128)} async-done(((f32[96,16,128]{2,0,1:T(8,128)}), f32[96,16,128]{2,0,1:T(8,128)}, u32[]{:S(2)}, u32[]{:S(2)}) %all-to-all-start) | async-done | bytes 786464 | tf_op jit(solution)/shard_map/all_to_all | solution.py:65
  265.4 1.2 reduce_sum.57
  266.6 0.8 copy.53
  267.4 5.4 %all-to-all-start.2 = ((f32[352,2,64]{0,2,1:T(8,128)}), f32[352,2,64]{0,2,1:T(8,128)S(1)}, u32[]{:S(2)}, u32[]{:S(2)}) async-start(f32[352,2,64]{0,2,1:T(8,128)} %bitcast.20), calls=%async_computation.4 | async-start | bytes 393216 | tf_op jit(solution)/shard_map/all_to_all | solution.py:78
  272.8 0.5 copy.43
  273.4 0.3 copy.42
  273.7 1.5 copy.55
  275.1 2.0 copy.54
  277.1 5.4 %all-to-all-done.2 = f32[352,2,64]{0,2,1:T(8,128)S(1)} async-done(((f32[352,2,64]{0,2,1:T(8,128)}), f32[352,2,64]{0,2,1:T(8,128)S(1)}, u32[]{:S(2)}, u32[]{:S(2)}) %all-to-all-start.2) | async-done | bytes 180256 | tf_op jit(solution)/shard_map/all_to_all | solution.py:78
  282.5 0.8 fusion.67
  283.4 11.3 %all_to_all.49 = bf16[2,2,352,64]{2,3,1,0:T(8,128)(2,1)S(1)} all-to-all(bf16[2,2,352,64]{2,3,1,0:T(8,128)(2,1)S(1)} %broadcast_in_dim.43), channel_id=1, replica_groups=mesh['zh'=2,'y'=4,'x'=4,'zl'=4,'c'=2] {'zh'}, dimensions={0} | all-to-all | bytes 360448 | tf_op jit(solution)/shard_map/all_to_all | solution.py:85
  294.8 0.2 copy.57
  295.0 0.6 broadcast_in_dim.45
  295.5 39.8 %all_to_all.50 = bf16[16,2,352,128]{3,2,1,0:T(8,128)(2,1)} all-to-all(bf16[16,2,352,128]{3,2,1,0:T(8,128)(2,1)S(1)} %broadcast_in_dim.45), channel_id=1, replica_groups=mesh['zh'=2,'y'=4,'x'=4,'zl'=4,'c'=2] {'y','x'}, dimensions={0} | all-to-all | bytes 5767168 | tf_op jit(solution)/shard_map/all_to_all | solution.py:89
  335.4 3.4 copy.58
  338.8 1.2 fusion.78
  339.9 2.3 fusion.77
  342.3 2.1 copy.66
  344.4 2.3 copy.61
  346.7 1.0 copy.67
  347.7 1.4 copy.62
  (26 shorter events, 0.2 us)
Async XLA Ops:
  7.2 3.1 copy-start
  7.2 3.1 copy-start.10
  7.2 75.1 %all-gather.3.cloned.1.call-start = ((), (), s32[]{:S(2)}) async-start(), calls=%async_computation.9 | async-start | bytes 12255232 | tf_op jit(solution)/shard_map/all_gather | solution.py:109
  10.2 185.2 %reduce-scatter.3.cloned.1.call-start = ((), (), s32[]{:S(2)}) async-start(), calls=%async_computation.7 | async-start | bytes 9437184 | tf_op jit(solution)/shard_map/reduce_scatter | solution.py:158
  87.2 1.0 copy-start.6
  94.9 1.0 copy-start.11
  96.7 1.5 copy-start.7
  97.3 1.0 copy-start.8
  103.9 1.2 copy-start.9
  103.9 137.2 %reduce-scatter.5.cloned.1.call-start = ((), (), s32[]{:S(2)}) async-start(), calls=%async_computation.8 | async-start | bytes 3538944 | tf_op jit(solution)/shard_map/reduce_scatter | solution.py:176
  196.8 1.2 copy-start.2
  202.5 41.5 %all-to-all-start.1 = ((f32[256,16,128]{2,0,1:T(8,128)}), f32[256,16,128]{2,0,1:T(8,128)S(1)}, u32[]{:S(2)}, u32[]{:S(2)}) async-start(f32[256,16,128]{2,0,1:T(8,128)} %copy_bitcast_fusion), calls=%async_computation.3 | async-start | bytes 4194304 | tf_op jit(solution)/shard_map/all_to_all | solution.py:65
  244.0 21.4 %all-to-all-start = ((f32[96,16,128]{2,0,1:T(8,128)}), f32[96,16,128]{2,0,1:T(8,128)}, u32[]{:S(2)}, u32[]{:S(2)}) async-start(f32[96,16,128]{2,0,1:T(8,128)} %copy_bitcast_fusion.1), calls=%async_computation.2 | async-start | bytes 1572864 | tf_op jit(solution)/shard_map/all_to_all | solution.py:65
  251.0 22.4 %copy-start.4 = (bf16[96,2048]{1,0:T(8,128)(2,1)S(1)}, bf16[96,2048]{1,0:T(8,128)(2,1)}, u32[]{:S(2)}) copy-start(bf16[96,2048]{1,0:T(8,128)(2,1)} %param.14) | copy-start | bytes 1179652
  267.4 15.1 %all-to-all-start.2 = ((f32[352,2,64]{0,2,1:T(8,128)}), f32[352,2,64]{0,2,1:T(8,128)S(1)}, u32[]{:S(2)}, u32[]{:S(2)}) async-start(f32[352,2,64]{0,2,1:T(8,128)} %bitcast.20), calls=%async_computation.4 | async-start | bytes 393216 | tf_op jit(solution)/shard_map/all_to_all | solution.py:78
  342.3 4.4 %copy-start.5 = (bf16[1,96,16,128]{1,3,2,0:T(8,128)(2,1)S(1)}, bf16[1,96,16,128]{1,3,2,0:T(8,128)(2,1)}, u32[]{:S(2)}) copy-start(bf16[1,96,16,128]{1,3,2,0:T(8,128)(2,1)} %get-tuple-element.16) | copy-start | bytes 1179652
  342.3 5.4 %copy-start.3 = (bf16[1,256,16,128]{1,3,2,0:T(8,128)(2,1)S(1)}, bf16[1,256,16,128]{1,3,2,0:T(8,128)(2,1)}, u32[]{:S(2)}) copy-start(bf16[1,256,16,128]{1,3,2,0:T(8,128)(2,1)} %get-tuple-element.14) | copy-start | bytes 3145732
  344.4 4.7 %copy-start.1 = (bf16[1,128,768]{2,1,0:T(8,128)(2,1)S(1)}, bf16[1,128,768]{2,1,0:T(8,128)(2,1)}, u32[]{:S(2)}) copy-start(bf16[1,128,768]{2,1,0:T(8,128)(2,1)} %param.11) | copy-start | bytes 589828
Sparse Core Ops, SparseCore 0:
  10.4 71.8 all-gather.2
  104.1 91.2 reduce-scatter.2
  197.9 43.1 reduce-scatter.4
where the time goes:
time: 357 us; the launch traced here: 356 us
  waiting for transfers between devices  193 us (54%)
  blocking collectives  51.2 us (14%)
  local copies, waits for them, and re-layouts  34.8 us (10%)
  matrix products  30.3 us (8%)
  starting transfers between devices  19.4 us (5%)
  between operations  14.1 us (4%)
  other arithmetic  12.7 us (4%)
    reduce_scatter x1, waiting for transfers between devices, shards(): lax.psum_scatter((scale_two * jnp.dot(active.T, embed_half, preferred_ele...  70.9 us
    all_gather x1, waiting for transfers between devices, gather_weights(): got = lax.all_gather(mine, ('zh',) + NARROW, axis=0, tiled=False)  70.6 us
    all_to_all x1, blocking collectives, wide_mean_update(): lax.all_to_all(jnp.broadcast_to(back[None], (n_plane,) + back.shape), pla...  39.8 us
    reduce_scatter x1, waiting for transfers between devices, shards(): lax.psum_scatter(term_first, NARROW, scatter_dimension=0, tiled=True)  31.8 us
    all_to_all x2, waiting for transfers between devices, plane_sum(): got = lax.all_to_all(delta, plane, 1, 0, tiled=True)  14.4 us
    all_to_all x2, starting transfers between devices, plane_sum(): got = lax.all_to_all(delta, plane, 1, 0, tiled=True)  13.7 us
    unnamed x30, local copies, waits for them, and re-layouts  12.1 us
    all_to_all x1, blocking collectives, wide_mean_update(): lax.all_to_all(jnp.broadcast_to(both[None], (n_half,) + both.shape), 'zh'...  11.3 us
  transfers between devices with their start and end apart: 6, of which 5 were waited for; matrix products, arithmetic and copies ran while one was open for 9% of the time, Pallas kernels for 0%

commit v1 on v0

--- a/solution.py
+++ b/solution.py
@@ -75,7 +75,9 @@
     p1 = cols // n_plane
     p2 = p1 // n_half
     part = plane_sum(delta) if part is None else part
-    got = lax.all_to_all(part, "zh", 1, 0, tiled=True)
+    got = jnp.concatenate(
+        lax.all_to_all(jnp.stack(jnp.split(part, lax.axis_size("zh"), axis=1)), "zh", 0, 0), axis=0
+    )
     mean = jnp.sum(got.reshape(n_half, rows, p2), axis=0) / sites
     start = lax.axis_index(plane) * p1 + lax.axis_index("zh") * p2
     mom_piece = lax.dynamic_slice_in_dim(momentum, start, p2, axis=1)

time: 357 us -> 357 us (level)
  no operation moved by 1% of the time
where the time goes in v1:
time: 357 us; the launch traced here: 356 us
  waiting for transfers between devices  193 us (54%)
  blocking collectives  51.4 us (14%)
  local copies, waits for them, and re-layouts  34.8 us (10%)
  matrix products  30.3 us (8%)
  starting transfers between devices  19.4 us (5%)
  between operations  14.1 us (4%)
  other arithmetic  12.8 us (4%)
    reduce_scatter x1, waiting for transfers between devices, shards(): lax.psum_scatter((scale_two * jnp.dot(active.T, embed_half, preferred_ele...  70.9 us
    all_gather x1, waiting for transfers between devices, gather_weights(): got = lax.all_gather(mine, ('zh',) + NARROW, axis=0, tiled=False)  70.6 us
    all_to_all x1, blocking collectives, wide_mean_update(): lax.all_to_all(jnp.broadcast_to(back[None], (n_plane,) + back.shape), pla...  40.1 us
    reduce_scatter x1, waiting for transfers between devices, shards(): lax.psum_scatter(term_first, NARROW, scatter_dimension=0, tiled=True)  31.8 us
    all_to_all x2, waiting for transfers between devices, plane_sum(): got = lax.all_to_all(delta, plane, 1, 0, tiled=True)  14.4 us
    all_to_all x2, starting transfers between devices, plane_sum(): got = lax.all_to_all(delta, plane, 1, 0, tiled=True)  13.7 us
    unnamed x30, local copies, waits for them, and re-layouts  12.1 us
    all_to_all x1, blocking collectives, wide_mean_update(): lax.all_to_all(jnp.broadcast_to(both[None], (n_half,) + both.shape), 'zh'...  11.3 us
  transfers between devices with their start and end apart: 6, of which 5 were waited for; matrix products, arithmetic and copies ran while one was open for 9% of the time, Pallas kernels for 0%

profile of v1, /device:TPU:96, one launch (start us, length us, event | category | flops | bytes accessed | tf_op | source)
XLA Modules:
  0.0 355.9 jit_solution(14589145628790348260)
XLA Ops:
  7.2 0.0 copy-start
  7.2 0.0 all-gather.3.cloned.1.call-start
  7.2 1.1 constant_dynamic-slice_fusion
  8.3 0.9 constant_dynamic-slice_fusion.1
  9.3 0.9 pad_maximum_fusion
  10.2 0.0 all-gather.3.cloned.1.call-update
  10.2 0.0 reduce-scatter.3.cloned.1.call-start
  10.3 1.2 gather_fusion
  11.5 0.2 copy.53
  11.7 70.6 %all-gather.3.cloned.1.call-done = bf16[2816,2048]{1,0:T(8,128)(2,1)} async-done(((bf16[176,2048]{1,0:T(8,128)(2,1)}), bf16[2816,2048]{1,0:T(8,128)(2,1)}) %all-gather.3.cloned.1.call-update) | async-done | bytes 11534352 | tf_op jit(solution)/shard_map/all_gather | solution.py:111
  82.3 4.8 %multiply_convert_fusion.3 = (bf16[256,2048]{1,0:T(8,128)(2,1)S(1)}, f32[256,2048]{1,0:T(8,128)}) fusion(bf16[2,8,176,2048]{3,2,1,0:T(8,128)(2,1)} %bitcast.99, bf16[256,8,2,48]{0,3,2,1:T(8,128)(2,1)S(1)} %bitcast.96, pred[256]{0:T(512)(128)(4,1)S(1)} %compare_and_fusion), kind=kOutput, calls=%fused_computation.35 | convolution fusion | flops 810745856 | bytes 6684928 | tf_op jit(solution)/shard_map/bnhr,hnrc->bc/dot_general | solution.py:140
  87.2 1.0 copy-done.6
  88.1 1.5 reshape.101
  89.7 5.2 %multiply_reduce_fusion.1 = (f32[256]{0:T(256)S(1)}, f32[256,2048]{1,0:T(8,128)S(1)}) fusion(bf16[2,8,176,2048]{3,2,1,0:T(8,128)(2,1)} %bitcast.100, bf16[256,8,2,128]{3,2,1,0:T(2,128)(2,1)} %reshape.101), kind=kOutput, calls=%fused_computation.34 | convolution fusion | flops 2149056256 | bytes 11535360 | tf_op jit(solution)/shard_map/bnhr,hnrc->bc/dot_general | solution.py:151
  94.9 0.0 copy-start.11
  94.9 0.6 convolution_multiply_fusion.1
  95.5 0.1 copy.56
  95.6 0.1 fusion.52
  95.7 0.2 fusion.53
  95.9 0.8 multiply_reduce_fusion
  96.7 0.5 multiply_convert_fusion.2
  97.3 0.0 copy-start.8
  97.3 1.0 copy-done.8
  98.2 5.7 %multiply_convert_fusion = bf16[2048,2048]{1,0:T(8,128)(2,1)} fusion(bf16[256,2048]{1,0:T(8,128)(2,1)S(1)} %copy-done.7, bf16[256,2048]{1,0:T(8,128)(2,1)S(1)} %multiply_convert_fusion.2), kind=kOutput, calls=%fused_computation.1 | convolution fusion | flops 2155872256 | bytes 10485760 | tf_op jit(solution)/shard_map/dot_general | solution.py:161
  103.9 0.0 reduce-scatter.3.cloned.1.call-update
  103.9 0.2 reduce-scatter.5.cloned.1.call-start
  104.1 1.0 copy-done.9
  105.1 7.1 %multiply_bitcast_fusion = f32[256,8,2,128]{0,3,1,2:T(8,128)} fusion(bf16[2,8,176,2048]{3,2,1,0:T(8,128)(2,1)} %bitcast.101, bf16[256,2048]{1,0:T(8,128)(2,1)S(1)} %copy-done.9), kind=kOutput, calls=%fused_computation.31 | convolution fusion | flops 2148007936 | bytes 11534336 | tf_op jit(solution)/shard_map/bc,hnrc->bnhr/dot_general | solution.py:168
  112.2 3.4 copy.57
  115.6 2.7 mul.261
  118.3 6.1 %multiply_convert_fusion.1 = bf16[768,2048]{1,0:T(8,128)(2,1)} fusion(f32[256,2048]{1,0:T(8,128)} %get-tuple-element.27, f32[256,2048]{1,0:T(8,128)} %mul.261, bf16[256,768]{1,0:T(8,128)(2,1)S(1)} %gather_fusion, pred[256]{0:T(512)(128)(4,1)S(1)} %compare_and_fusion), kind=kOutput, calls=%fused_computation.6 | convolution fusion | flops 819134464 | bytes 7733504 | tf_op jit(solution)/shard_map/dot_general | solution.py:173
  124.4 70.9 %reduce-scatter.3.cloned.1.call-done = bf16[256,2048]{1,0:T(8,128)(2,1)} async-done(((bf16[2048,2048]{1,0:T(8,128)(2,1)}), bf16[256,2048]{1,0:T(8,128)(2,1)}) %reduce-scatter.3.cloned.1.call-update) | async-done | bytes 1048592 | tf_op jit(solution)/shard_map/reduce_scatter | solution.py:160
  195.4 1.5 convert_element_type.78
  196.8 0.0 copy-start.2
  196.8 0.0 reduce-scatter.5.cloned.1.call-update
  196.9 1.2 copy-done.2
  198.1 4.4 %copy_bitcast_fusion = f32[256,16,128]{2,0,1:T(8,128)} fusion(bf16[256,2048]{1,0:T(8,128)(2,1)S(1)} %copy-done.2, f32[256,2048]{1,0:T(8,128)S(1)} %convert_element_type.78, bf16[1,256,2048]{2,1,0:T(8,128)(2,1)} %param.19, bf16[1,256,2048]{2,1,0:T(8,128)(2,1)} %param.17), kind=kLoop, calls=%fused_computation.29 | loop fusion | flops 7864320 | bytes 7340032 | tf_op jit(solution)/shard_map/all_to_all | solution.py:65
  202.5 6.8 %all-to-all-start.1 = ((f32[256,16,128]{2,0,1:T(8,128)}), f32[256,16,128]{2,0,1:T(8,128)S(1)}, u32[]{:S(2)}, u32[]{:S(2)}) async-start(f32[256,16,128]{2,0,1:T(8,128)} %copy_bitcast_fusion), calls=%async_computation.3 | async-start | bytes 4194304 | tf_op jit(solution)/shard_map/all_to_all | solution.py:65
  209.3 31.8 %reduce-scatter.5.cloned.1.call-done = bf16[96,2048]{1,0:T(8,128)(2,1)} async-done(((bf16[768,2048]{1,0:T(8,128)(2,1)}), bf16[96,2048]{1,0:T(8,128)(2,1)}) %reduce-scatter.5.cloned.1.call-update) | async-done | bytes 393232 | tf_op jit(solution)/shard_map/reduce_scatter | solution.py:178
  241.2 2.8 copy_bitcast_fusion.1
  244.0 6.8 %all-to-all-start = ((f32[96,16,128]{2,0,1:T(8,128)}), f32[96,16,128]{2,0,1:T(8,128)}, u32[]{:S(2)}, u32[]{:S(2)}) async-start(f32[96,16,128]{2,0,1:T(8,128)} %copy_bitcast_fusion.1), calls=%async_computation.2 | async-start | bytes 1572864 | tf_op jit(solution)/shard_map/all_to_all | solution.py:65
  250.9 0.1 reduce_sum.58
  251.0 14.4 %all-to-all-done = f32[96,16,128]{2,0,1:T(8,128)} async-done(((f32[96,16,128]{2,0,1:T(8,128)}), f32[96,16,128]{2,0,1:T(8,128)}, u32[]{:S(2)}, u32[]{:S(2)}) %all-to-all-start) | async-done | bytes 786464 | tf_op jit(solution)/shard_map/all_to_all | solution.py:65
  265.4 1.2 reduce_sum.57
  266.6 0.1 maximum_bitcast_fusion
  266.8 0.8 copy.60
  267.6 5.4 %all-to-all-start.2 = ((f32[2,352,64]{1,2,0:T(8,128)}), f32[2,352,64]{1,2,0:T(8,128)S(1)}, u32[]{:S(2)}, u32[]{:S(2)}) async-start(f32[2,352,64]{1,2,0:T(8,128)} %copy.60), calls=%async_computation.4 | async-start | bytes 393216 | tf_op jit(solution)/shard_map/all_to_all | solution.py:79
  273.0 0.5 copy.52
  273.5 0.3 copy.51
  273.8 1.5 copy.62
  275.3 2.0 copy.61
  277.3 5.3 %all-to-all-done.2 = f32[2,352,64]{1,2,0:T(8,128)S(1)} async-done(((f32[2,352,64]{1,2,0:T(8,128)}), f32[2,352,64]{1,2,0:T(8,128)S(1)}, u32[]{:S(2)}, u32[]{:S(2)}) %all-to-all-start.2) | async-done | bytes 180256 | tf_op jit(solution)/shard_map/all_to_all | solution.py:79
  282.6 0.8 fusion.68
  283.5 11.3 %all_to_all.41 = bf16[2,2,352,64]{2,3,1,0:T(8,128)(2,1)S(1)} all-to-all(bf16[2,2,352,64]{2,3,1,0:T(8,128)(2,1)S(1)} %broadcast_in_dim.43), channel_id=1, replica_groups=mesh['zh'=2,'y'=4,'x'=4,'zl'=4,'c'=2] {'zh'}, dimensions={0} | all-to-all | bytes 360448 | tf_op jit(solution)/shard_map/all_to_all | solution.py:87
  294.9 0.2 copy.64
  295.1 0.6 broadcast_in_dim.45
  295.6 40.1 %all_to_all.42 = bf16[16,2,352,128]{3,2,1,0:T(8,128)(2,1)} all-to-all(bf16[16,2,352,128]{3,2,1,0:T(8,128)(2,1)S(1)} %broadcast_in_dim.45), channel_id=1, replica_groups=mesh['zh'=2,'y'=4,'x'=4,'zl'=4,'c'=2] {'y','x'}, dimensions={0} | all-to-all | bytes 5767168 | tf_op jit(solution)/shard_map/all_to_all | solution.py:91
  335.7 3.4 copy.65
  339.1 1.2 fusion.79
  340.3 2.3 fusion.78
  342.6 2.1 copy.73
  344.7 2.3 copy.68
  347.0 1.0 copy.74
  348.0 1.4 copy.69
  (27 shorter events, 0.2 us)
Async XLA Ops:
  7.2 3.1 copy-start
  7.2 3.1 copy-start.10
  7.2 75.1 %all-gather.3.cloned.1.call-start = ((), (), s32[]{:S(2)}) async-start(), calls=%async_computation.9 | async-start | bytes 12255232 | tf_op jit(solution)/shard_map/all_gather | solution.py:111
  10.2 185.2 %reduce-scatter.3.cloned.1.call-start = ((), (), s32[]{:S(2)}) async-start(), calls=%async_computation.7 | async-start | bytes 9437184 | tf_op jit(solution)/shard_map/reduce_scatter | solution.py:160
  87.2 1.0 copy-start.6
  94.9 1.0 copy-start.11
  96.7 1.5 copy-start.7
  97.3 1.0 copy-start.8
  103.9 1.2 copy-start.9
  103.9 137.2 %reduce-scatter.5.cloned.1.call-start = ((), (), s32[]{:S(2)}) async-start(), calls=%async_computation.8 | async-start | bytes 3538944 | tf_op jit(solution)/shard_map/reduce_scatter | solution.py:178
  196.8 1.2 copy-start.2
  202.5 41.5 %all-to-all-start.1 = ((f32[256,16,128]{2,0,1:T(8,128)}), f32[256,16,128]{2,0,1:T(8,128)S(1)}, u32[]{:S(2)}, u32[]{:S(2)}) async-start(f32[256,16,128]{2,0,1:T(8,128)} %copy_bitcast_fusion), calls=%async_computation.3 | async-start | bytes 4194304 | tf_op jit(solution)/shard_map/all_to_all | solution.py:65
  244.0 21.4 %all-to-all-start = ((f32[96,16,128]{2,0,1:T(8,128)}), f32[96,16,128]{2,0,1:T(8,128)}, u32[]{:S(2)}, u32[]{:S(2)}) async-start(f32[96,16,128]{2,0,1:T(8,128)} %copy_bitcast_fusion.1), calls=%async_computation.2 | async-start | bytes 1572864 | tf_op jit(solution)/shard_map/all_to_all | solution.py:65
  266.6 6.9 %copy-start.4 = (bf16[96,2048]{1,0:T(8,128)(2,1)S(1)}, bf16[96,2048]{1,0:T(8,128)(2,1)}, u32[]{:S(2)}) copy-start(bf16[96,2048]{1,0:T(8,128)(2,1)} %param.14) | copy-start | bytes 1179652
  267.6 15.0 %all-to-all-start.2 = ((f32[2,352,64]{1,2,0:T(8,128)}), f32[2,352,64]{1,2,0:T(8,128)S(1)}, u32[]{:S(2)}, u32[]{:S(2)}) async-start(f32[2,352,64]{1,2,0:T(8,128)} %copy.60), calls=%async_computation.4 | async-start | bytes 393216 | tf_op jit(solution)/shard_map/all_to_all | solution.py:79
  342.6 4.4 %copy-start.5 = (bf16[1,96,16,128]{1,3,2,0:T(8,128)(2,1)S(1)}, bf16[1,96,16,128]{1,3,2,0:T(8,128)(2,1)}, u32[]{:S(2)}) copy-start(bf16[1,96,16,128]{1,3,2,0:T(8,128)(2,1)} %get-tuple-element.20) | copy-start | bytes 1179652
  342.6 5.4 %copy-start.3 = (bf16[1,256,16,128]{1,3,2,0:T(8,128)(2,1)S(1)}, bf16[1,256,16,128]{1,3,2,0:T(8,128)(2,1)}, u32[]{:S(2)}) copy-start(bf16[1,256,16,128]{1,3,2,0:T(8,128)(2,1)} %get-tuple-element.18) | copy-start | bytes 3145732
  344.7 4.7 %copy-start.1 = (bf16[1,128,768]{2,1,0:T(8,128)(2,1)S(1)}, bf16[1,128,768]{2,1,0:T(8,128)(2,1)}, u32[]{:S(2)}) copy-start(bf16[1,128,768]{2,1,0:T(8,128)(2,1)} %param.11) | copy-start | bytes 589828
Sparse Core Ops, SparseCore 0:
  10.4 71.8 all-gather.2
  104.0 91.2 reduce-scatter.2
  197.9 43.1 reduce-scatter.4
